TPU v7x, 128 devices: a whole 4x4x4 slice. The times are simulated.
128 devices in a mesh: group: 8 (over z, core), pair: 16 (over y, x).
Axes of the slice: x: 4, y: 4, z: 4, core: 2. Of those that a mesh axis runs over, the one named last changes fastest.
Arguments:
- query_embed: bfloat16 [8, 16, 1024], P('group'), may hold values from -6 to 6
- teacher_scores: float32 [8, 16, 16, 32], P('group', 'pair'), may hold values from -9 to 9
- pair_owner: int32 [8, 16, 16, 32, 1], P('group', 'pair'), may hold values from 0 to 127; in each aligned block of 512 rows (0 to 511, 512 to 1023, ..., all dimensions but the last counted through in order) at most 8 rows name the same one
- pair_row: int32 [8, 16, 16, 32], P('group', 'pair'), may hold values from 0 to 2047
- passage_hidden: bfloat16 [262144, 1024], P(('group', 'pair')), may hold values from -24 to 24
- projection: bfloat16 [1024, 1024], replicated, may hold values from -0.1875 to 0.1875
Outputs:
- query_loss: float32 [8, 16], P('group', 'pair')
- query_grad: float32 [8, 16, 1024], P('group', 'pair')
- hidden_grad: bfloat16 [262144, 1024], P(('group', 'pair'))
- projection_grad: float32 [1024, 1024], P(('group', 'pair'))
Inputs may be any that keep to these rules, and one draw needn't show every extreme that they name: `pair_owner`: owners are numbered with group as the slower index. Among the 512 candidates held by one device, at most 8 name the same owner, and every draw has a device and an owner with exactly 8. `pair_row`: A passage may be named by several candidates.
All inputs are finite; a program needn't handle non-finite values.
Results may differ from a plain program's by a relative error of at most 0.022.
Values may be sent and summed in bfloat16 or wider, within the bound.
A program may use at most 128 MiB of HBM per device.

v0:
```python
import math
import jax
import jax.numpy as jnp
from jax import lax
from jax.sharding import PartitionSpec as P

loss_scale = 1024.0


def soft_steps(values_all, values_own):
    return jax.nn.sigmoid((values_all[:, None, :] - values_own[:, :, None]) * 2.0)


def score_slope(soft_step, grad_all, grad_own):
    slopes = soft_step * (1.0 - soft_step)
    return 2.0 * (jnp.sum(slopes * grad_all[:, None, :], -1) - grad_own * jnp.sum(slopes, -1))


def shards(query_embed, teacher_scores, pair_owner, pair_row, passage_hidden, projection):
    model_width = query_embed.shape[2]
    query_rows = query_embed.shape[1]
    cand_dev = teacher_scores.shape[3]
    pass_rows = passage_hidden.shape[0]
    pair_size = lax.axis_size("pair")
    group_size = lax.axis_size("group")
    devices = pair_size * group_size
    cand_all = cand_dev * pair_size
    pair_count = query_rows * cand_dev
    capacity = max(2, 2 * pair_count // devices)
    query_dev = query_rows // pair_size
    inv_root = 1.0 / math.sqrt(model_width)
    spearman_den = float(cand_all * (cand_all * cand_all - 1))
    embedded = jnp.dot(passage_hidden, projection, preferred_element_type=jnp.float32).astype(
        jnp.bfloat16
    )
    owner_dev = pair_owner.reshape(pair_count)
    row_index = pair_row.reshape(pair_count)
    owner_marks = (owner_dev[:, None] == jnp.arange(devices, dtype=jnp.int32)[None, :]).astype(
        jnp.int32
    )
    slot_index = jnp.sum(jnp.cumsum(owner_marks, axis=0) * owner_marks, axis=1) - 1
    requests = jnp.zeros((devices, capacity), jnp.int32).at[owner_dev, slot_index].set(row_index)
    queries = query_embed[0]
    asked_rows = lax.all_to_all(
        requests, ("group", "pair"), split_axis=0, concat_axis=0, tiled=True
    )
    vectors = jnp.take(embedded, asked_rows, axis=0)
    replies = lax.all_to_all(vectors, ("group", "pair"), split_axis=0, concat_axis=0, tiled=True)
    pair_vectors = replies[owner_dev, slot_index].reshape(query_rows, cand_dev, model_width)
    scores = (
        jnp.einsum("qd,qcd->qc", queries, pair_vectors, preferred_element_type=jnp.float32)
        * inv_root
    )
    teacher_own = teacher_scores.reshape(query_rows, cand_dev)
    scores_all, teacher_all = (
        lax.all_gather(scores, "pair", axis=1, tiled=True),
        lax.all_gather(teacher_own, "pair", axis=1, tiled=True),
    )
    soft_step = soft_steps(scores_all, scores)
    rank_student = 0.5 + jnp.sum(soft_step, -1)
    rank_teacher = 0.5 + jnp.sum(soft_steps(teacher_all, teacher_own), -1)
    rank_gap = rank_student - rank_teacher
    loss_part = 6.0 * jnp.sum(rank_gap * rank_gap, axis=1) / spearman_den
    rank_grad = loss_scale * 12.0 * rank_gap / spearman_den
    grad_all = lax.all_gather(rank_grad, "pair", axis=1, tiled=True)
    score_grad = score_slope(soft_step, grad_all, rank_grad)
    query_part = (
        jnp.sum(score_grad[:, :, None] * pair_vectors.astype(jnp.float32), axis=1) * inv_root
    )
    pair_grad = (
        score_grad[:, :, None] * queries.astype(jnp.float32)[:, None, :] * inv_root
    ).astype(jnp.bfloat16)
    query_sum, loss_own = (
        lax.psum_scatter(
            query_part.astype(jnp.bfloat16), "pair", scatter_dimension=0, tiled=True
        ).astype(jnp.float32),
        lax.psum_scatter(
            loss_part.astype(jnp.bfloat16), "pair", scatter_dimension=0, tiled=True
        ).astype(jnp.float32),
    )
    outgoing = (
        jnp.zeros((devices, capacity, model_width), jnp.bfloat16)
        .at[owner_dev, slot_index]
        .set(pair_grad.reshape(pair_count, model_width))
    )
    arrived = lax.all_to_all(outgoing, ("group", "pair"), split_axis=0, concat_axis=0, tiled=True)
    embed_grad = (
        jnp.zeros((pass_rows, model_width), jnp.float32)
        .at[asked_rows.reshape(-1)]
        .add(arrived.reshape(-1, model_width).astype(jnp.float32))
    )
    grad_rounded = embed_grad.astype(jnp.bfloat16)
    hidden_grad = jnp.einsum(
        "pe,de->pd", grad_rounded, projection, preferred_element_type=jnp.float32
    ).astype(jnp.bfloat16)
    projection_grad = lax.psum_scatter(
        jnp.einsum("pr,pe->re", passage_hidden, grad_rounded, preferred_element_type=jnp.float32),
        ("group", "pair"),
        scatter_dimension=0,
        tiled=True,
    )
    return (
        loss_own.reshape(1, query_dev),
        query_sum.reshape(1, query_dev, model_width),
        hidden_grad,
        projection_grad,
    )


def solution(mesh):
    placed = (
        P("group", None, None),
        P("group", "pair", None, None),
        P("group", "pair", None, None, None),
        P("group", "pair", None, None),
        P(("group", "pair"), None),
        P(),
    )
    return jax.shard_map(
        shards,
        mesh=mesh,
        in_specs=placed,
        out_specs=(
            P("group", "pair"),
            P("group", "pair", None),
            P(("group", "pair"), None),
            P(("group", "pair"), None),
        ),
        check_vma=False,
    )
```

profile of v0, /device:TPU:0, one launch (start us, length us, event | category | flops | bytes accessed | tf_op | source)
XLA Modules:
  0.0 964.4 jit_solution(8039499689911197415)
XLA Ops:
  7.2 0.0 copy-start
  7.2 0.9 eq.25
  8.1 0.8 eq.29
  8.9 0.8 reshape.243
  9.7 0.5 broadcast.268
  10.2 1.4 reduce.10
  11.5 0.1 reshape.209
  11.6 0.1 copy.29
  11.7 0.2 fusion.12
  12.0 0.2 fusion.11
  12.3 22.0 %scatter_fusion = s32[128,8]{0,1:T(8,128)S(1)} fusion(s32[128,8]{0,1:T(8,128)S(1)} %broadcast_in_dim.18, s32[512]{0:T(512)S(1)} %bitcast.82, s32[512]{0:T(512)S(1)} %reshape.243), kind=kCustom, calls=%fused_computation.2 | custom fusion | bytes 10240 | tf_op jit(solution)/shard_map/scatter | solution.py:42
  34.3 0.7 copy.31
  35.0 11.1 %all-to-all-start = ((s32[128,1,8]{2,1,0:T(1,128)}), s32[128,1,8]{2,1,0:T(1,128)S(1)}, u32[]{:S(2)}, u32[]{:S(2)}) async-start(s32[128,1,8]{2,1,0:T(1,128)} %copy.31), calls=%async_computation | async-start | bytes 131072 | tf_op jit(solution)/shard_map/all_to_all | solution.py:44
  46.2 0.0 copy-done
  46.2 8.3 convolution_convert_fusion.1
  54.5 1.2 all-to-all-done
  55.7 0.1 copy.33
  55.9 0.1 reshape.229
  56.0 8.8 gather_fusion
  64.7 0.0 copy-start.2
  64.7 0.0 copy-start.1
  64.7 3.2 bitcast_select_fusion
  67.9 9.1 all-to-all-start.1
  77.1 0.0 copy-done.2
  77.1 0.1 copy.35
  77.1 41.4 %all-gather = f32[1,1,16,512]{2,1,0,3:T(1,128)S(1)} all-gather(f32[1,1,16,32]{2,1,0,3:T(1,128)S(1)} %copy.35), channel_id=2, replica_groups=mesh['group'=8,'pair'=16] {'pair'}, dimensions={3}, use_global_device_ids=true | all-gather | bytes 34816 | tf_op jit(solution)/shard_map/all_gather | solution.py:57
  118.5 0.1 copy.36
  118.6 0.0 copy-done.1
  118.6 0.4 fusion.8
  119.1 0.0 all-to-all-done.1
  119.1 7.7 gather_fusion.1
  126.8 0.4 fusion.15
  127.2 22.0 %all-gather.1 = f32[16,32,16]{1,2,0:T(8,128)S(1)} all-gather(f32[1,32,16]{1,2,0:T(8,128)S(1)} %get-tuple-element.28), channel_id=1, replica_groups=mesh['group'=8,'pair'=16] {'pair'}, dimensions={0}, use_global_device_ids=true | all-gather | bytes 34816 | tf_op jit(solution)/shard_map/all_gather | solution.py:56
  149.3 0.1 reshape.264
  149.4 0.6 fusion.9
  149.9 22.6 %all-gather.2 = f32[16,32,16]{1,2,0:T(8,128)S(1)} all-gather(f32[1,32,16]{1,2,0:T(8,128)S(1)} %multiply_bitcast_fusion), channel_id=1, replica_groups=mesh['group'=8,'pair'=16] {'pair'}, dimensions={0}, use_global_device_ids=true | all-gather | bytes 34816 | tf_op jit(solution)/shard_map/all_gather | solution.py:65
  172.6 0.1 reshape.266
  172.7 0.5 multiply_reduce_fusion.1
  173.2 0.1 subtract_multiply_fusion.1
  173.3 0.1 reshape.226
  173.4 1.2 fusion.5
  174.7 1.6 broadcast_in_dim.23
  176.2 73.0 %scatter_fusion.1 = bf16[128,8,1024]{2,1,0:T(8,128)(2,1)} fusion(bf16[128,8,1024]{2,1,0:T(8,128)(2,1)} %broadcast_in_dim.23, s32[512]{0:T(512)S(1)} %bitcast.83, bf16[512,1024]{1,0:T(8,128)(2,1)} %fusion.5), kind=kCustom, calls=%fused_computation.3 | custom fusion | bytes 3149824 | tf_op jit(solution)/shard_map/scatter | solution.py:84
  249.2 8.3 all-to-all-start.2
  257.5 0.0 reduce-scatter.4.cloned.1.call-start
  257.6 0.8 reduce.11
  258.4 0.1 reshape.218
  258.5 28.3 %all-to-all-done.2 = bf16[128,8,1024]{2,1,0:T(8,128)(2,1)} async-done(((bf16[128,8,1024]{2,1,0:T(8,128)(2,1)}), bf16[128,8,1024]{2,1,0:T(8,128)(2,1)}, u32[]{:S(2)}, u32[]{:S(2)}) %all-to-all-start.2) | async-done | bytes 2097184 | tf_op jit(solution)/shard_map/all_to_all | solution.py:86
  286.8 13.4 %scatter_custom_fusion.2 = f32[2048,1024]{1,0:T(8,128)} fusion(s32[1024]{0:T(1024)S(1)} %bitcast.101, f32[]{:T(128)} %constant.26.clone.1, bf16[128,8,1024]{2,1,0:T(8,128)(2,1)} %all-to-all-done.2), kind=kCustom, calls=%fused_computation.5 | custom fusion | flops 2097152 | bytes 10485764 | tf_op jit(solution)/shard_map/scatter-add | solution.py:90
  300.2 11.2 %convolution_bitcast_fusion = f32[1024,1024]{0,1:T(8,128)} fusion(bf16[2048,1024]{1,0:T(8,128)(2,1)} %param.10, f32[2048,1024]{1,0:T(8,128)} %scatter_custom_fusion.2), kind=kOutput, calls=%fused_computation.10 | convolution fusion | flops 4297064448 | bytes 16777216 | tf_op jit(solution)/shard_map/pr,pe->re/dot_general | solution.py:97
  311.3 5.3 copy.41
  316.7 0.0 copy-start.3
  316.7 0.0 reduce-scatter.4.cloned.1.call-update
  316.7 0.5 multiply_reduce_fusion
  317.3 0.1 copy-done.3
  317.3 0.6 dynamic-slice
  317.9 72.1 %all-reduce.2 = (bf16[16]{0:T(256)(128)(2,1)S(1)}, bf16[16,1024]{1,0:T(8,128)(2,1)S(1)}) all-reduce(bf16[16]{0:T(256)(128)(2,1)S(1)} %multiply_convert_fusion.1, bf16[16,1024]{1,0:T(8,128)(2,1)S(1)} %multiply_convert_fusion), channel_id=3, replica_groups=mesh['group'=8,'pair'=16] {'pair'}, use_global_device_ids=true, to_apply=%region_7.8.clone | all-reduce | flops 16400 | bytes 65600
  390.0 1.2 dynamic-slice.1
  391.9 1.2 bitcast_convert_fusion.1
  393.2 9.5 convolution_convert_fusion
  402.6 553.7 %reduce-scatter.4.cloned.1.call-done = f32[8,1024]{1,0:T(8,128)} async-done(((f32[1024,1024]{1,0:T(8,128)}), f32[8,1024]{1,0:T(8,128)}) %reduce-scatter.4.cloned.1.call-update) | async-done | bytes 32784
  (21 shorter events, 0.3 us)
Async XLA Ops:
  7.2 39.0 %copy-start = (bf16[1024,1024]{1,0:T(8,128)(2,1)S(1)}, bf16[1024,1024]{1,0:T(8,128)(2,1)}, u32[]{:S(2)}) copy-start(bf16[1024,1024]{1,0:T(8,128)(2,1)} %param.11) | copy-start | bytes 6291460
  35.0 20.6 %all-to-all-start = ((s32[128,1,8]{2,1,0:T(1,128)}), s32[128,1,8]{2,1,0:T(1,128)S(1)}, u32[]{:S(2)}, u32[]{:S(2)}) async-start(s32[128,1,8]{2,1,0:T(1,128)} %copy.31), calls=%async_computation | async-start | bytes 131072 | tf_op jit(solution)/shard_map/all_to_all | solution.py:44
  64.7 12.3 %copy-start.2 = (f32[1,1,16,32]{3,2,1,0:T(8,128)S(1)}, f32[1,1,16,32]{3,2,1,0:T(8,128)}, u32[]{:S(2)}) copy-start(f32[1,1,16,32]{3,2,1,0:T(8,128)} %param.7) | copy-start | bytes 6148
  64.7 53.9 %copy-start.1 = (bf16[1,16,1024]{2,1,0:T(8,128)(2,1)S(1)}, bf16[1,16,1024]{2,1,0:T(8,128)(2,1)}, u32[]{:S(2)}) copy-start(bf16[1,16,1024]{2,1,0:T(8,128)(2,1)} %param.6) | copy-start | bytes 98308
  67.9 51.1 %all-to-all-start.1 = ((bf16[128,8,1024]{2,1,0:T(8,128)(2,1)}), bf16[128,8,1024]{2,1,0:T(8,128)(2,1)}, u32[]{:S(2)}, u32[]{:S(2)}) async-start(bf16[128,8,1024]{2,1,0:T(8,128)(2,1)} %bitcast_select_fusion), calls=%async_computation.1 | async-start | bytes 4194304 | tf_op jit(solution)/shard_map/all_to_all | solution.py:48
  249.2 37.6 %all-to-all-start.2 = ((bf16[128,8,1024]{2,1,0:T(8,128)(2,1)}), bf16[128,8,1024]{2,1,0:T(8,128)(2,1)}, u32[]{:S(2)}, u32[]{:S(2)}) async-start(bf16[128,8,1024]{2,1,0:T(8,128)(2,1)} %scatter_fusion.1), calls=%async_computation.2 | async-start | bytes 4194304 | tf_op jit(solution)/shard_map/all_to_all | solution.py:86
  257.5 698.9 %reduce-scatter.4.cloned.1.call-start = ((), (), s32[]{:S(2)}) async-start(), calls=%async_computation.4 | async-start | bytes 4227072
  316.7 0.7 copy-start.3
Sparse Core Ops, SparseCore 0:
  316.8 639.5 reduce-scatter.3
where the time goes:
time: 968 us; the launch traced here: 964 us
  waiting for transfers between devices  583 us (60%)
  blocking collectives  158 us (16%)
  local copies, waits for them, and re-layouts  125 us (13%)
  matrix products  29.3 us (3%)
  starting transfers between devices  28.6 us (3%)
  other arithmetic  24 us (2%)
  between operations  16.1 us (2%)
    unnamed x2, waiting for transfers between devices  554 us
    scatter x1, local copies, waits for them, and re-layouts, shards(): outgoing = jnp.zeros((devices, capacity, model_width), jnp.bfloat16).at[o...  73 us
    unnamed x1, blocking collectives  72.1 us
    all_gather x1, blocking collectives, shards(): lax.all_gather(teacher_own, 'pair', axis=1, tiled=True)  41.4 us
    all_to_all x1, waiting for transfers between devices, shards(): lax.all_to_all(outgoing, ('group', 'pair'), split_axis=0, concat_axis=0,...  28.3 us
    all_gather x1, blocking collectives, shards(): grad_all = lax.all_gather(rank_grad, 'pair', axis=1, tiled=True)  22.6 us
    all_gather x1, blocking collectives, shards(): lax.all_gather(scores, 'pair', axis=1, tiled=True)  22 us
    scatter x1, local copies, waits for them, and re-layouts, shards(): jnp.zeros((devices, capacity), jnp.int32).at[owner_dev, slot_index]  22 us
  transfers between devices with their start and end apart: 4, of which 3 were waited for; matrix products, arithmetic and copies ran while one was open for 2% of the time, Pallas kernels for 0%

commit v1 on v0

--- a/solution.py
+++ b/solution.py
@@ -5,6 +5,11 @@
 from jax.sharding import PartitionSpec as P
 
 loss_scale = 1024.0
+
+
+def gather_over(x, name, along):
+    outgoing = jnp.stack([x] * lax.axis_size(name))
+    return jnp.concatenate(lax.all_to_all(outgoing, name, 0, 0), axis=along)
 
 
 def soft_steps(values_all, values_own):
@@ -53,7 +58,7 @@
     )
     teacher_own = teacher_scores.reshape(query_rows, cand_dev)
     scores_all, teacher_all = (
-        lax.all_gather(scores, "pair", axis=1, tiled=True),
+        gather_over(scores, "pair", 1),
         lax.all_gather(teacher_own, "pair", axis=1, tiled=True),
     )
     soft_step = soft_steps(scores_all, scores)

time: 968 us -> 966 us (level)
    all_to_all x0 -> x1, blocking collectives: none -> 38.2 us  [shards(): lax.all_to_all(vectors, ('group', 'pair'), split_axis=0, concat_axis=0, t...]
    all_gather x1 -> x0, blocking collectives: 22 us -> none  [shards(): lax.all_gather(scores, 'pair', axis=1, tiled=True)]
    all_gather x1, blocking collectives: 41.4 us -> 24 us  [shards(): lax.all_gather(teacher_own, 'pair', axis=1, tiled=True)]
where the time goes in v1:
time: 966 us; the launch traced here: 962 us
  waiting for transfers between devices  583 us (60%)
  blocking collectives  157 us (16%)
  local copies, waits for them, and re-layouts  128 us (13%)
  matrix products  29.3 us (3%)
  other arithmetic  26.2 us (3%)
  starting transfers between devices  21.5 us (2%)
  between operations  16.1 us (2%)
    unnamed x2, waiting for transfers between devices  554 us
    scatter x1, local copies, waits for them, and re-layouts, shards(): outgoing = jnp.zeros((devices, capacity, model_width), jnp.bfloat16).at[o...  73 us
    unnamed x1, blocking collectives  72.1 us
    all_to_all x1, blocking collectives, shards(): lax.all_to_all(vectors, ('group', 'pair'), split_axis=0, concat_axis=0, t...  38.2 us
    all_to_all x1, waiting for transfers between devices, shards(): lax.all_to_all(outgoing, ('group', 'pair'), split_axis=0, concat_axis=0,...  28.3 us
    all_gather x1, blocking collectives, shards(): lax.all_gather(teacher_own, 'pair', axis=1, tiled=True)  24 us
    all_gather x1, blocking collectives, shards(): grad_all = lax.all_gather(rank_grad, 'pair', axis=1, tiled=True)  23.1 us
    scatter x1, local copies, waits for them, and re-layouts, shards(): jnp.zeros((devices, capacity), jnp.int32).at[owner_dev, slot_index]  22 us
  transfers between devices with their start and end apart: 4, of which 3 were waited for; matrix products, arithmetic and copies ran while one was open for 2% of the time, Pallas kernels for 0%

profile of v1, /device:TPU:0, one launch (start us, length us, event | category | flops | bytes accessed | tf_op | source)
XLA Modules:
  0.0 962.0 jit_solution(1709333063075192004)
XLA Ops:
  7.2 0.0 copy-start
  7.2 0.9 eq.25
  8.1 0.8 eq.29
  8.9 0.8 reshape.249
  9.7 0.5 broadcast.269
  10.2 1.4 reduce.10
  11.5 0.1 reshape.214
  11.6 0.1 copy.38
  11.7 0.2 fusion.12
  12.0 0.2 fusion.11
  12.3 22.0 %scatter_fusion = s32[128,8]{0,1:T(8,128)S(1)} fusion(s32[128,8]{0,1:T(8,128)S(1)} %broadcast_in_dim.18, s32[512]{0:T(512)S(1)} %bitcast.76, s32[512]{0:T(512)S(1)} %reshape.249), kind=kCustom, calls=%fused_computation.2 | custom fusion | bytes 10240 | tf_op jit(solution)/shard_map/scatter | solution.py:47
  34.3 0.7 copy.40
  35.0 11.1 %all-to-all-start = ((s32[128,1,8]{2,1,0:T(1,128)}), s32[128,1,8]{2,1,0:T(1,128)S(1)}, u32[]{:S(2)}, u32[]{:S(2)}) async-start(s32[128,1,8]{2,1,0:T(1,128)} %copy.40), calls=%async_computation | async-start | bytes 131072 | tf_op jit(solution)/shard_map/all_to_all | solution.py:49
  46.2 0.0 copy-done
  46.2 8.3 convolution_convert_fusion.1
  54.4 1.2 all-to-all-done
  55.7 0.1 copy.42
  55.9 0.1 reshape.235
  56.0 8.8 gather_fusion
  64.7 1.9 bitcast_select_fusion
  66.6 38.2 %all_to_all.30 = bf16[128,8,1024]{2,1,0:T(8,128)(2,1)} all-to-all(bf16[128,8,1024]{2,1,0:T(8,128)(2,1)S(1)} %bitcast_select_fusion), channel_id=1, replica_groups=mesh['group'=8,'pair'=16] {'group','pair'}, dimensions={0} | all-to-all | bytes 4194304 | tf_op jit(solution)/shard_map/all_to_all | solution.py:53
  104.8 7.7 gather_fusion.1
  112.5 0.0 copy-done.1
  112.5 0.4 fusion.15
  112.9 0.7 reshape.301
  113.7 4.2 all-to-all-start.2
  117.8 0.0 copy-done.5
  117.9 0.7 copy.44
  118.5 24.0 %all-gather = f32[1,1,16,512]{2,1,0,3:T(1,128)S(1)} all-gather(f32[1,1,16,32]{2,1,0,3:T(1,128)} %copy.44), channel_id=2, replica_groups=mesh['group'=8,'pair'=16] {'pair'}, dimensions={3}, use_global_device_ids=true | all-gather | bytes 34816 | tf_op jit(solution)/shard_map/all_gather | solution.py:62
  142.6 0.7 copy.45
  143.3 0.0 all-to-all-done.2
  143.3 0.5 broadcast.276
  143.8 1.5 reduce.12
  145.3 0.1 reshape.302
  145.4 0.1 sub.58
  145.5 1.5 fusion.8
  147.1 0.0 copy-start.3
  147.1 0.6 copy-done.3
  147.7 0.0 copy-done.4
  147.7 23.1 %all-gather.1 = f32[16,32,16]{1,2,0:T(8,128)S(1)} all-gather(f32[1,32,16]{1,2,0:T(8,128)S(1)} %multiply_bitcast_fusion), channel_id=1, replica_groups=mesh['group'=8,'pair'=16] {'pair'}, dimensions={0}, use_global_device_ids=true | all-gather | bytes 34816 | tf_op jit(solution)/shard_map/all_gather | solution.py:70
  170.9 0.1 reshape.270
  171.0 1.4 fusion.9
  172.3 0.8 subtract_multiply_fusion.1
  173.2 0.1 reshape.232
  173.2 1.2 fusion.5
  174.5 1.6 broadcast_in_dim.40
  176.0 73.0 %scatter_fusion.1 = bf16[128,8,1024]{2,1,0:T(8,128)(2,1)} fusion(bf16[128,8,1024]{2,1,0:T(8,128)(2,1)} %broadcast_in_dim.40, s32[512]{0:T(512)S(1)} %bitcast.77, bf16[512,1024]{1,0:T(8,128)(2,1)} %fusion.5), kind=kCustom, calls=%fused_computation.3 | custom fusion | bytes 3149824 | tf_op jit(solution)/shard_map/scatter | solution.py:89
  249.0 6.2 all-to-all-start.3
  255.2 0.0 reduce-scatter.4.cloned.1.call-start
  255.3 0.8 reduce.11
  256.1 0.1 reshape.224
  256.2 28.3 %all-to-all-done.3 = bf16[128,8,1024]{2,1,0:T(8,128)(2,1)} async-done(((bf16[128,8,1024]{2,1,0:T(8,128)(2,1)}), bf16[128,8,1024]{2,1,0:T(8,128)(2,1)}, u32[]{:S(2)}, u32[]{:S(2)}) %all-to-all-start.3) | async-done | bytes 2097184 | tf_op jit(solution)/shard_map/all_to_all | solution.py:91
  284.5 13.4 %scatter_custom_fusion.2 = f32[2048,1024]{1,0:T(8,128)} fusion(s32[1024]{0:T(1024)S(1)} %bitcast.94, f32[]{:T(128)} %constant.26.clone.1, bf16[128,8,1024]{2,1,0:T(8,128)(2,1)} %all-to-all-done.3), kind=kCustom, calls=%fused_computation.5 | custom fusion | flops 2097152 | bytes 10485764 | tf_op jit(solution)/shard_map/scatter-add | solution.py:95
  297.9 11.2 %convolution_bitcast_fusion = f32[1024,1024]{0,1:T(8,128)} fusion(bf16[2048,1024]{1,0:T(8,128)(2,1)} %param.10, f32[2048,1024]{1,0:T(8,128)} %scatter_custom_fusion.2), kind=kOutput, calls=%fused_computation.10 | convolution fusion | flops 4297064448 | bytes 16777216 | tf_op jit(solution)/shard_map/pr,pe->re/dot_general | solution.py:102
  309.0 5.3 copy.50
  314.4 0.0 reduce-scatter.4.cloned.1.call-update
  314.4 0.5 multiply_reduce_fusion
  315.0 0.1 copy-done.6
  315.0 0.6 dynamic-slice
  315.6 72.1 %all-reduce.2 = (bf16[16]{0:T(256)(128)(2,1)S(1)}, bf16[16,1024]{1,0:T(8,128)(2,1)S(1)}) all-reduce(bf16[16]{0:T(256)(128)(2,1)S(1)} %multiply_convert_fusion.1, bf16[16,1024]{1,0:T(8,128)(2,1)S(1)} %multiply_convert_fusion), channel_id=3, replica_groups=mesh['group'=8,'pair'=16] {'pair'}, use_global_device_ids=true, to_apply=%region_7.8.clone | all-reduce | flops 16400 | bytes 65600
  387.7 1.2 dynamic-slice.1
  389.6 1.2 bitcast_convert_fusion.1
  390.8 9.5 convolution_convert_fusion
  400.3 553.7 %reduce-scatter.4.cloned.1.call-done = f32[8,1024]{1,0:T(8,128)} async-done(((f32[1024,1024]{1,0:T(8,128)}), f32[8,1024]{1,0:T(8,128)}) %reduce-scatter.4.cloned.1.call-update) | async-done | bytes 32784
  (28 shorter events, 0.4 us)
Async XLA Ops:
  7.2 39.0 %copy-start = (bf16[1024,1024]{1,0:T(8,128)(2,1)S(1)}, bf16[1024,1024]{1,0:T(8,128)(2,1)}, u32[]{:S(2)}) copy-start(bf16[1024,1024]{1,0:T(8,128)(2,1)} %param.11) | copy-start | bytes 6291460
  35.0 20.6 %all-to-all-start = ((s32[128,1,8]{2,1,0:T(1,128)}), s32[128,1,8]{2,1,0:T(1,128)S(1)}, u32[]{:S(2)}, u32[]{:S(2)}) async-start(s32[128,1,8]{2,1,0:T(1,128)} %copy.40), calls=%async_computation | async-start | bytes 131072 | tf_op jit(solution)/shard_map/all_to_all | solution.py:49
  104.8 7.7 copy-start.1
  104.8 13.1 %copy-start.5 = (f32[1,1,16,32]{3,2,1,0:T(8,128)S(1)}, f32[1,1,16,32]{3,2,1,0:T(8,128)}, u32[]{:S(2)}) copy-start(f32[1,1,16,32]{3,2,1,0:T(8,128)} %param.7) | copy-start | bytes 6148
  113.7 29.6 %all-to-all-start.2 = ((f32[16,1,512]{2,1,0:T(1,128)}), f32[16,1,512]{2,1,0:T(1,128)}, u32[]{:S(2)}, u32[]{:S(2)}) async-start(f32[16,1,512]{2,1,0:T(1,128)} %reshape.301), calls=%async_computation.2 | async-start | bytes 65536 | tf_op jit(solution)/shard_map/all_to_all | solution.py:12
  145.5 1.6 copy-start.2
  147.1 0.6 copy-start.3
  147.1 0.6 copy-start.4
  249.0 35.5 %all-to-all-start.3 = ((bf16[128,8,1024]{2,1,0:T(8,128)(2,1)}), bf16[128,8,1024]{2,1,0:T(8,128)(2,1)}, u32[]{:S(2)}, u32[]{:S(2)}) async-start(bf16[128,8,1024]{2,1,0:T(8,128)(2,1)} %scatter_fusion.1), calls=%async_computation.3 | async-start | bytes 4194304 | tf_op jit(solution)/shard_map/all_to_all | solution.py:91
  255.2 698.8 %reduce-scatter.4.cloned.1.call-start = ((), (), s32[]{:S(2)}) async-start(), calls=%async_computation.5 | async-start | bytes 4227072
  314.4 0.7 copy-start.6
Sparse Core Ops, SparseCore 0:
  314.5 639.4 reduce-scatter.3
